TPU v7x, 32 devices: a whole 2x2x4 slice. The times are simulated.
32 devices in a mesh: dp: 16 (over z, y, core), mp: 2 (over x).
Axes of the slice: x: 2, y: 2, z: 4, core: 2. Of those that a mesh axis runs over, the one named last changes fastest.
Arguments:
- layer_input: bfloat16 [24576, 768], P(('dp', 'mp')), may hold values from -6 to 6
- gain_attn: bfloat16 [768], replicated, may hold values from 0.5 to 1.5
- w_query: bfloat16 [768, 768], P(None, 'mp'), may hold values from -0.3125 to 0.3125
- w_key: bfloat16 [768, 768], P(None, 'mp'), may hold values from -0.21875 to 0.21875
- w_value: bfloat16 [768, 768], P(None, 'mp'), may hold values from -0.21875 to 0.21875
- w_out: bfloat16 [768, 768], P('mp'), may hold values from -0.875 to 0.875
- gain_mlp: bfloat16 [768], replicated, may hold values from 0.5 to 1.5
- w_gate: bfloat16 [768, 2048], P(None, 'mp'), may hold values from -0.21875 to 0.21875
- w_up: bfloat16 [768, 2048], P(None, 'mp'), may hold values from -0.21875 to 0.21875
- w_down: bfloat16 [2048, 768], P('mp'), may hold values from -0.125 to 0.125
- segment_start: int32 [16, 7], P('dp'), may hold values from 0 to 1472, as said below
- segment_parent: int32 [16, 7], P('dp'), may hold values from 0 to 2, as said below
- out_grad: bfloat16 [24576, 768], P(('dp', 'mp')), may hold values from -6 to 6
Outputs:
- output: float32 [24576, 768], P(('dp', 'mp'))
- input_grad: float32 [24576, 768], P(('dp', 'mp'))
- gain_attn_grad: float32 [768], replicated
- w_query_grad: float32 [768, 768], P(None, 'mp')
- w_key_grad: float32 [768, 768], P(None, 'mp')
- w_value_grad: float32 [768, 768], P(None, 'mp')
- w_out_grad: float32 [768, 768], P('mp')
- gain_mlp_grad: float32 [768], replicated
- w_gate_grad: float32 [768, 2048], P(None, 'mp')
- w_up_grad: float32 [768, 2048], P(None, 'mp')
- w_down_grad: float32 [2048, 768], P('mp')
Inputs may be any that keep to these rules, and one draw needn't show every extreme that they name: `segment_start`: per tree the segments are stored in order trunk, two branches, four leaves; starts rise strictly from 0, every branch or leaf has 64 to 192 tokens, and the last leaf has exactly 64. `segment_parent`: segment 0 is the trunk (entry 0), segments 1 and 2 have parent 0, and each of them is the parent of exactly two of segments 3 to 6.
All inputs are finite; a program needn't handle non-finite values.
Results may differ from a plain program's by a relative error of at most 0.018.
Values may be sent and summed in bfloat16 or wider, within the bound.
A program may use at most 192 MiB of HBM per device.

v0:
```python
import functools
import math

import jax
import jax.numpy as jnp
from jax import lax
from jax.experimental import pallas as pl
from jax.experimental.pallas import tpu as pltpu
from jax.sharding import Mesh
from jax.sharding import PartitionSpec as P

BF = jnp.bfloat16
F32 = jnp.float32
HD=64; EPS=1e-5; BIG=-1e30
C_Q = (HD**-0.5)*math.log2(math.e)
LN2 = math.log(2.0)
NT=(((1,),(1,)),((),())); NN=(((1,),(0,)),((),())); TN=(((0,),(0,)),((),()))
def dot(a,b,dims=NN): return lax.dot_general(a,b,dims,preferred_element_type=F32)
def lanes(shape): return lax.broadcasted_iota(jnp.int32, shape, 1)

def split3(x):
    hi=x.astype(BF).astype(F32); r=x-hi; mid=r.astype(BF).astype(F32); lo=r-mid
    return hi,mid,lo

def tables(starts, parents, row0, rows, nseg, tree_len):
    sh=(rows,128)
    t = row0 + lax.broadcasted_iota(jnp.int32, sh, 0)
    st=[starts[0,s] for s in range(nseg)]+[tree_len]
    par=[parents[0,s] for s in range(nseg)]
    ln=[st[s+1]-st[s] for s in range(nseg)]
    def pick(vals, idx):
        r = vals[0]
        for s in range(1,nseg): r = jnp.where(idx==s, vals[s], r)
        return r
    D=[]
    gps=[]
    for s in range(nseg):
        p=par[s]; gp=pick(par,p); gps.append(gp)
        off=jnp.where(p!=s, pick(ln,p), 0)+jnp.where((gp!=s)&(gp!=p), pick(ln,gp), 0)
        D.append(off-st[s])
    seg=jnp.zeros(sh,jnp.int32); pos=t+D[0]
    for s in range(1,nseg):
        ge=t>=st[s]
        seg=seg+ge.astype(jnp.int32)
        pos=pos+jnp.where(ge, D[s]-D[s-1], 0)
    f=lanes(sh)-64
    parl=jnp.zeros((1,128),jnp.int32)-1; gpl=parl
    fl=lanes((1,128))-64
    for s in range(nseg):
        parl=jnp.where(fl==s, par[s], parl); gpl=jnp.where(fl==s, gps[s], gpl)
    vis=(f==seg)|(parl==seg)|(gpl==seg)|(f<0)|(f>=nseg)
    qf=jnp.where(f==seg,1.0,0.0)
    kf=jnp.where(vis,0.0,BIG)
    kf=jnp.where((f>=8)&(f<11),1.0,kf)
    return pos.astype(F32), qf, kf

def rot_tables(posf):
    l=lax.broadcasted_iota(jnp.int32,(1,128),1)
    fr=jnp.exp((l%32).astype(F32)*(-2.0*math.log(10000.0)/HD))
    ang=posf*fr
    sg=jnp.where((l%64)<32,-1.0,1.0)
    return jnp.cos(ang), jnp.sin(ang)*sg

def swap32(x):
    l=lanes(x.shape)
    return jnp.where((l&32)==0, pltpu.roll(x,96,1), pltpu.roll(x,32,1))


MESH=pl.DeviceIdType.MESH
RING=8
def ring_chip(r):
    return jnp.where(r<RING//2, 2*r, 2*(RING-1-r)+1)
def chip_ring(n):
    return jnp.where(n%2==0, n//2, RING-1-n//2)

class Place:
    def __init__(self):
        self.core=lax.axis_index("core"); self.mp=lax.axis_index("mp")
        self.pos=chip_ring(lax.axis_index("chip"))
        self.nxt=[ring_chip(lax.rem(self.pos+1,RING)), ring_chip(lax.rem(self.pos+RING-1,RING))]
    def barrier(self):
        b=pltpu.get_barrier_semaphore()
        ds=[{"core":1-self.core},{"mp":1-self.mp},{"chip":self.nxt[0]},{"chip":self.nxt[1]}]
        for d in ds: pl.semaphore_signal(b, inc=1, device_id=d, device_id_type=MESH)
        pl.semaphore_wait(b, len(ds))

def copy_to(src,dst,sems,k,dev):
    return pltpu.make_async_remote_copy(src,dst,sems.at[0,k],sems.at[1,k],device_id=dev,device_id_type=MESH)

class Gather:
    def __init__(self,p,src,out,kinds,sems):
        self.p,self.src,self.out,self.kinds,self.sems=p,src,out,kinds,sems
    def ref(self,x,a,ch,core=None):
        n=self.out[a].shape[0]//(2*RING)
        return x[a].at[pl.ds(pl.multiple_of((self.p.core*RING+ch)*n,n),n)]
    def at(self,d,dist): return lax.rem(self.p.pos+(dist if d==0 else RING-dist),RING)
    def hops(self,a,d): return 4-self.kinds[a] if d==0 else 3+self.kinds[a]
    def cp(self,src,dst,a,k,dev):
        return pltpu.make_async_remote_copy(src,dst,self.sems.at[0,a,k],self.sems.at[1,a,k],device_id=dev,device_id_type=MESH)
    def cx(self,a): return self.cp(self.ref(self.src,a,self.p.pos),self.ref(self.out,a,self.p.pos),a,0,{"mp":1-self.p.mp})
    def cag(self,a,d,t):
        r=self.ref(self.out,a,self.at(1-d,t))
        return self.cp(r,r,a,1+4*d+t,{"chip":self.p.nxt[d]})
    def cfc(self,a,d,t):
        r=self.ref(self.out,a,self.at(1-d,t+1))
        return self.cp(r,r,a,9+4*d+t,{"core":1-self.p.core})
    def cfo(self,a):
        r=self.ref(self.out,a,self.p.pos)
        return self.cp(r,r,a,17,{"core":1-self.p.core})
    def agstart(self,a):
        self.cx(a).wait()
        for d in range(2): self.cag(a,d,0).start()
        self.cfo(a).start()
    def ag(self,a,t):
        for d in range(2):
            if t<self.hops(a,d):
                self.cag(a,d,t).wait()
                if t+1<self.hops(a,d): self.cag(a,d,t+1).start()
                self.cfc(a,d,t).start()
    def finish(self,a):
        self.cfo(a).wait()
        for d in range(2):
            for t in range(self.hops(a,d)): self.cfc(a,d,t).wait()

def front_kernel(nseg,starts,parents,x_ref,gain,wq,wk,wv,*refs):
    refs=list(refs)
    def take(n):
        r=refs[:n]; del refs[:n]; return r
    NW=(len(refs)-21)//2
    src=take(NW)
    big=take(7); heads,hrecv=take(2); out=take(NW)
    x_peer,normed,cos_o,sin_o,ke,ve,qe,qf_s,kf_s,sems,wsems,osem=take(12)
    at=Place(); mp=at.mp
    R=x_ref.shape[0]; T=2*R; B=256; nh=wq.shape[1]//HD
    G=Gather(at,src,out,[a%2 for a in range(NW)],wsems)
    mine=pl.multiple_of(mp*R,R); theirs=pl.multiple_of((1-mp)*R,R)
    at.barrier()
    peer={"mp":1-mp}
    NG=NW
    for a in range(NG): G.cx(a).start()
    c_x=copy_to(x_ref,x_peer,sems,0,peer); c_x.start()
    for a in range(NG,NW): G.cx(a).start()
    def tab(c,_):
        r0=pl.multiple_of(c*B,B); rows=pl.ds(r0,B)
        posf,qf,kf=tables(starts,parents,r0,B,nseg,T)
        co,si=rot_tables(posf)
        cos_o[rows,:]=co; sin_o[rows,:]=si
        qf_s[rows,:]=qf.astype(BF); kf_s[rows,:]=kf.astype(BF)
        return 0
    lb=lanes((B,128)); low=lb<64
    vone=jnp.where((lb>=64)&(lb<67),1.0,0.0)
    def proj(xr,base):
        def f(c,_):
            rows=pl.ds(pl.multiple_of(base+c*B,B),B)
            x=xr[pl.ds(pl.multiple_of(c*B,B),B),:].astype(F32)
            r1=lax.rsqrt(jnp.mean(x*x,axis=1,keepdims=True)+EPS)
            n=(x*r1*gain[0:1]).astype(BF)
            normed[rows,:]=n
            co=cos_o[rows,:]; si=sin_o[rows,:]; qf=qf_s[rows,:].astype(F32); kf=kf_s[rows,:].astype(F32)
            qq=dot(n,wq[...]); kk=dot(n,wk[...]); vv=dot(n,wv[...])
            for p in range(nh//2):
                cs=slice(128*p,128*p+128)
                q=qq[:,cs]; k=kk[:,cs]; v=vv[:,cs]
                q=(q*co+swap32(q)*si)*C_Q; k=k*co+swap32(k)*si
                for hh in range(2):
                    if hh: q=pltpu.roll(q,64,1); k=pltpu.roll(k,64,1); v=pltpu.roll(v,64,1)
                    qe[2*p+hh,rows,:]=jnp.where(low,q,qf).astype(BF)
                    ke[2*p+hh,rows,:]=jnp.where(low,k,kf).astype(BF)
                    ve[2*p+hh,rows,:]=jnp.where(low,v,vone).astype(BF)
            return 0
        lax.fori_loop(0,R//B,f,0)
    for a in range(NG): G.agstart(a)
    lax.fori_loop(0,T//B,tab,0)
    for a in range(NG): G.ag(a,0)
    proj(x_ref,mine)
    for a in range(NG): G.ag(a,1)
    c_x.wait()
    proj(x_peer,theirs)
    puts=[pltpu.make_async_copy(s,d,osem.at[i]) for i,(s,d) in enumerate(zip((x_peer,normed,cos_o,sin_o,ke,ve),big))]
    for q in puts: q.start()
    for a in range(NG): G.ag(a,2)
    def put_q(p): return pltpu.make_async_copy(qe.at[pl.ds(2*p,2)],big[6].at[pl.ds(2*p,2)],osem.at[6+p])
    causal=lax.broadcasted_iota(jnp.int32,(B,B),1)<=lax.broadcasted_iota(jnp.int32,(B,B),0)
    def c_h(p):
        cs=pl.ds(pl.multiple_of(p*128,128),128)
        return pltpu.make_async_remote_copy(heads.at[pl.ds(theirs,R),cs],hrecv.at[:,cs],sems.at[0,1+p],sems.at[1,1+p],device_id=peer,device_id_type=MESH)
    def attend(p,_):
        cs=pl.ds(pl.multiple_of(p*128,128),128)
        for i in range(T//B):
            n=(i+1)*B; rows=slice(i*B,(i+1)*B)
            outs=[]
            for hh in range(2):
                h=2*p+hh
                q=qe[h,rows,:]
                s=dot(q,ke[h,0:n,:],NT)
                sd=jnp.where(causal,s[:,n-B:],BIG)
                s=sd if i==0 else jnp.concatenate([s[:,:n-B],sd],axis=1)
                m=jnp.max(s,axis=1,keepdims=True)
                pr=jnp.exp2(s-m).astype(BF)
                o=dot(pr,ve[h,0:n,:])
                den=o[:,64:65]
                o=o*(1.0/den)
                a,b,c=split3(-(m+jnp.log2(den)))
                qe[h,rows,:]=jnp.where(lb==72,a,jnp.where(lb==73,b,jnp.where(lb==74,c,q.astype(F32)))).astype(BF)
                outs.append(o)
            heads[rows,cs]=jnp.where(low,outs[0],pltpu.roll(outs[1],64,1)).astype(BF)
            if i==3:
                @pl.when(p==1)
                def _():
                    for a in range(NG): G.ag(a,3)
        c_h(p).start()
        put_q(p).start()
        return 0
    lax.fori_loop(0,nh//2,attend,0)
    for a in range(NW): G.finish(a)
    for q in puts: q.wait()
    for p in range(nh//2): put_q(p).wait()
    for p in range(nh//2): c_h(p).wait()

def front(x,gain,wq,wk,wv,starts,parents,weights,cid):
    R,Dm=x.shape; T=2*R; H=wq.shape[1]; nh=H//HD; nseg=starts.shape[1]; NW=len(weights)
    Vs=pl.BlockSpec(memory_space=pltpu.VMEM); S=pl.BlockSpec(memory_space=pltpu.SMEM); N=pl.BlockSpec(memory_space=pl.ANY)
    sd=jax.ShapeDtypeStruct; hT=sd((nh,T,128),BF); V=pltpu.VMEM
    return pl.pallas_call(functools.partial(front_kernel,nseg),
        out_shape=(sd((R,Dm),BF),sd((T,Dm),BF),sd((T,128),F32),sd((T,128),F32),hT,hT,hT,sd((T,H),BF),sd((R,H),BF))+tuple(sd(w.shape,BF) for w in weights),
        in_specs=[S,S]+[Vs]*5+[N]*NW, out_specs=(N,)*7+(Vs,)*2+(N,)*NW,
        scratch_shapes=[V((R,Dm),BF),V((T,Dm),BF),V((T,128),F32),V((T,128),F32),V((nh,T,128),BF),V((nh,T,128),BF),V((nh,T,128),BF),V((T,128),BF),V((T,128),BF),
            pltpu.SemaphoreType.DMA((2,1+nh//2)),pltpu.SemaphoreType.DMA((2,NW,18)),pltpu.SemaphoreType.DMA((6+nh//2,))],
        compiler_params=pltpu.CompilerParams(collective_id=cid,has_side_effects=True,vmem_limit_bytes=67043328),
        name="attention_forward")(starts,parents,x,gain,wq,wk,wv,*weights)

class Ring:
    def __init__(self, shapes, kinds, count, gslots, swaps, early=True, slot=None):
        self.shapes,self.count,self.gslots,self.swaps,self.early=shapes,count,gslots,swaps,early
        self.slot=slot or (lambda u: lax.rem(u,gslots))
        self.nr=(len(swaps) if early else count) if swaps else count
        self.na=len(shapes); self.flows=[]
        for a,parts in enumerate(kinds):
            for c0,nc,k in parts:
                self.flows+=[(a,c0,nc,0,4-k),(a,c0,nc,1,3+k)]
        self.nf=len(self.flows)
        self.own=[s[0] for s in swaps] if swaps else list(range(count))
        self.nv=len(self.own)
        na,nf=self.na,self.nf
        self.k_rs=na; self.k_x=0; self.k_ag=na; self.k_fc=self.k_ag+4*nf; self.k_fo=self.k_fc+4*nf; self.k_put=self.k_fo+na
        self.n1=na+4*nf; self.n2=self.k_put+na
    def scratch(self):
        V=pltpu.VMEM; U=self.count
        s=[V((self.gslots,2,RING)+x,BF) for x in self.shapes] if self.gslots else []
        s+=[V((U,RING)+x,BF) for x in self.shapes]
        s+=[V((self.nr,)+x,BF) for x in self.shapes]
        s+=[V((self.nv,)+((RING,)+x if self.early else x),BF) for x in self.shapes] if self.swaps else []
        s+=[V((self.nr,h,self.shapes[a][0],nc),BF) for a,c0,nc,d,h in self.flows]
        return s+[pltpu.SemaphoreType.DMA((2,U,self.n1)),pltpu.SemaphoreType.DMA((2,self.nv,self.n2))]
    def bind(self,p,dst,sc,g=None):
        self.p,self.dst=p,dst
        sc=list(sc); na=self.na
        if g is None: g,sc=sc[:na],sc[na:]
        self.g=g; self.r=sc[:na]; self.fin=sc[na:2*na]; sc=sc[2*na:]
        if self.swaps: self.xr=sc[:na]; sc=sc[na:]
        self.arr=sc[:self.nf]; self.sem,self.sem2=sc[self.nf:]
        return self
    def at(self,d,dist):
        return lax.rem(self.p.pos+(dist if d==0 else RING-dist),RING)
    def cp(self,src,dst,u,k,dev):
        return pltpu.make_async_remote_copy(src,dst,self.sem.at[0,u,k],self.sem.at[1,u,k],device_id=dev,device_id_type=MESH)
    def cp2(self,src,dst,v,k,dev):
        return pltpu.make_async_remote_copy(src,dst,self.sem2.at[0,v,k],self.sem2.at[1,v,k],device_id=dev,device_id_type=MESH)
    def c1(self,u,a): return self.cp(self.g[a].at[self.slot(u),1-self.p.core],self.r[a].at[u],u,a,{"core":1-self.p.core})
    def start(self,u):
        for a in range(self.na): self.c1(u,a).start()
    def uown(self,v): return self.own[v] if self.swaps else v
    def u_of(self,w): return self.uown(w) if self.early else w
    def w_own(self,v): return v if self.early else self.uown(v)
    def crs(self,w,f,t):
        a,c0,nc,d,h=self.flows[f]
        src=self.r[a].at[self.u_of(w),self.at(d,h),:,pl.ds(c0,nc)] if t==0 else self.arr[f].at[w,t-1]
        return self.cp(src,self.arr[f].at[w,t],self.u_of(w),self.k_rs+4*f+t,{"chip":self.p.nxt[d]})
    def cx(self,v,a): return self.cp2(self.r[a].at[self.swaps[v][1]] if self.early else self.fin[a].at[self.swaps[v][1]],self.xr[a].at[v],v,self.k_x+a,{"mp":1-self.p.mp})
    def push(self,v):
        u=self.swaps[v][1]
        for a in range(self.na):
            self.c1(u,a).wait()
            r,g=self.r[a],self.g[a]
            def add(s,_):
                r[u,s]=r[u,s]+g[self.slot(u),self.p.core,s]; return 0
            lax.fori_loop(0,RING,add,0)
            self.cx(v,a).start()
    def xstart(self,v):
        for a in range(self.na): self.cx(v,a).start()
    def first(self,v):
        u=self.u_of(v)
        for a in range(self.na):
            self.c1(u,a).wait()
            if self.swaps and self.early: self.cx(v,a).wait()
            r,g=self.r[a],self.g[a]
            def add(s,_):
                t=r[u,s].astype(F32)+g[self.slot(u),self.p.core,s].astype(F32)
                if self.swaps and self.early: t=t+self.xr[a][v,s].astype(F32)
                r[u,s]=t.astype(BF); return 0
            lax.fori_loop(0,RING,add,0)
            for f in range(self.nf):
                if self.flows[f][0]==a: self.crs(v,f,0).start()
    def rs(self,v,t):
        u=self.u_of(v)
        for f,(a,c0,nc,d,h) in enumerate(self.flows):
            if t<h:
                self.crs(v,f,t).wait()
                if t+1<h:
                    self.arr[f][v,t]=self.arr[f][v,t]+self.r[a][u,self.at(d,h-t-1),:,pl.ds(c0,nc)]
                    self.crs(v,f,t+1).start()
        if t==3:
            for f in range(0,self.nf,2):
                a,c0,nc,d,h=self.flows[f]; h2=self.flows[f+1][4]
                w=self.r[a][u,self.p.pos,:,pl.ds(c0,nc)].astype(F32)+self.arr[f][v,h-1].astype(F32)+self.arr[f+1][v,h2-1].astype(F32)
                self.fin[a][v,:,pl.ds(c0,nc)]=w.astype(BF)
    def cag(self,v,f,t):
        a,c0,nc,d,h=self.flows[f]
        dst=self.dst(v,a,self.at(1-d,t)).at[:,pl.ds(c0,nc)]
        src=self.fin[a].at[self.w_own(v),:,pl.ds(c0,nc)] if t==0 else dst
        return self.cp2(src,dst,v,self.k_ag+4*f+t,{"chip":self.p.nxt[d]})
    def cfc(self,v,f,t):
        a,c0,nc,d,h=self.flows[f]
        ref=self.dst(v,a,self.at(1-d,t+1)).at[:,pl.ds(c0,nc)]
        return self.cp2(ref,ref,v,self.k_fc+4*f+t,{"core":1-self.p.core})
    def cfo(self,v,a): return self.cp2(self.fin[a].at[self.w_own(v)],self.dst(v,a,self.p.pos),v,self.k_fo+a,{"core":1-self.p.core})
    def put(self,v,a): return pltpu.make_async_copy(self.fin[a].at[self.w_own(v)],self.dst(v,a,self.p.pos),self.sem2.at[0,v,self.k_put+a])
    def agstart(self,v):
        for a in range(self.na):
            if not self.early:
                u=self.uown(v)
                self.cx(v,a).wait()
                self.fin[a][u]=self.fin[a][u]+self.xr[a][v]
            for f in range(self.nf):
                if self.flows[f][0]==a: self.cag(v,f,0).start()
            self.cfo(v,a).start(); self.put(v,a).start()
    def ag(self,v,t):
        for f,(a,c0,nc,d,h) in enumerate(self.flows):
            if t<h:
                self.cag(v,f,t).wait()
                if t+1<h: self.cag(v,f,t+1).start()
                self.cfc(v,f,t).start()
    def finish(self,v):
        for a in range(self.na):
            self.put(v,a).wait(); self.cfo(v,a).wait()
        for f,(a,c0,nc,d,h) in enumerate(self.flows):
            for t in range(h): self.cfc(v,f,t).wait()

SHAPES_M,KINDS_M=[(48,1536)],[[(0,768,0),(768,768,1)]]
RING_M=Ring(SHAPES_M,KINDS_M,2,2,[(1,0)],True,lambda u: 0)
RING_N=Ring(SHAPES_M,KINDS_M,2,0,[(1,0)],False,lambda u: 1)
RING_O=Ring([(48,384)],[[(0,256,0),(256,128,1)]],2,2,[(1,0)])
RING_C=Ring([(48,384)],[[(0,256,0),(256,128,1)]],3,3,[])
def main_kernel(nM,nN,nO,nC,*refs):
    refs=list(refs)
    def take(n):
        r=refs[:n]; del refs[:n]; return r
    x_ref,og,heads,hrecv,wo,wop,gain_a,gain_m=take(8)
    wg_h,wu_h,wd_h,wgp_h,wup_h,wdp_h,qe_h,ke_h,ve_h,co_h,si_h,norm_h,xp_h,wq_h,wk_h,wv_h=take(16)
    out_h,ig_h=take(2); outM=take(1); outO=take(1); outC=take(1); gains_out,=take(1)
    scM=take(nM); scN=take(nN); scO=take(nO); scC=take(nC)
    dhs,dh,res,snd,rcv,gx,gring,sems,lsem,wsem=take(10)
    at=Place(); mp=at.mp
    R,Dm=x_ref.shape; T=2*R; nh=qe_h.shape[0]; B=256; nb=T//B; H=wo.shape[0]; F=512
    core=at.core
    def dst_m(q): return lambda v,a,ch: outM[0].at[q,core,ch]
    def dst_c(v,a,ch): return outC[0].at[v,core,ch]
    M=RING_M.bind(at,dst_m(0),scM); N=RING_N.bind(at,dst_m(1),scN,M.g); O=RING_O.bind(at,lambda v,a,ch: outO[0].at[core,ch],scO); C=RING_C.bind(at,dst_c,scC)
    mine=pl.multiple_of(mp*R,R); theirs=pl.multiple_of((1-mp)*R,R)
    W=R//3
    def blk(i): return pl.ds(i*W,W)
    at.barrier()
    c_dh=copy_to(dhs,dh.at[pl.ds(mine,R)],sems,0,{"mp":1-mp})

    def mlp(n2,n2t,ogt,acc,dn2,hid,dg,du,wgb,wub,wdb):
        def loads(g,u,d,q,slot):
            cs=pl.ds(pl.multiple_of(q*F,F),F)
            return [pltpu.make_async_copy(g.at[:,cs],wgb.at[slot],wsem.at[slot,0]),
                    pltpu.make_async_copy(u.at[:,cs],wub.at[slot],wsem.at[slot,1]),
                    pltpu.make_async_copy(d.at[cs,:],wdb.at[slot],wsem.at[slot,2])]
        for q in loads(wgp_h,wup_h,wdp_h,0,0): q.start()
        def pre(i,_):
            rows=pl.ds(pl.multiple_of(i*W,W),W); mr=pl.ds(pl.multiple_of(mine+i*W,W),W)
            r=x_ref[rows,:].astype(F32)+dot(heads[mr,:],wo[...])+dot(hrecv[rows,:],wop[...])
            res[rows,:]=r
            n=(r*lax.rsqrt(jnp.mean(r*r,axis=1,keepdims=True)+EPS)*gain_m[1:2]).astype(BF)
            n2[rows,:]=n
            n2t[:,rows]=n.T
            ogt[:,rows]=og[rows,:].T
            return 0
        lax.fori_loop(0,3,pre,0)
        acc[...]=jnp.zeros_like(acc); dn2[...]=jnp.zeros_like(dn2)
        def step(c,_):
            slot=lax.rem(c,2)
            for q in loads(wg_h,wu_h,wd_h,0,slot): q.wait()
            @pl.when(c==0)
            def _():
                for q in loads(wgp_h,wup_h,wdp_h,1,1): q.start()
            @pl.when((c>0)&(c<3))
            def _():
                for q in loads(wg_h,wu_h,wd_h,c-1,1-slot): q.start()
            wg,wu,wd=wgb[slot],wub[slot],wdb[slot]
            def half(i,_):
                rows=pl.ds(pl.multiple_of(i*W,W),W)
                gate=dot(n2[rows,:],wgb[slot]); up=dot(n2[rows,:],wub[slot]); dhid=dot(og[rows,:],wdb[slot],NT)
                sg=1.0/(1.0+jnp.exp(-gate)); silu=gate*sg
                hid[rows,:]=(silu*up).astype(BF)
                dg[rows,:]=(dhid*up*sg*(1.0+gate*(1.0-sg))).astype(BF)
                du[rows,:]=(dhid*silu).astype(BF)
                return 0
            lax.fori_loop(0,3,half,0)
            @pl.when(c==1)
            def _(): M.push(0)
            @pl.when(c==2)
            def _(): N.first(0)
            def back(i,_):
                rows=pl.ds(pl.multiple_of(i*W,W),W)
                acc[rows,:]=acc[rows,:]+dot(hid[rows,:],wdb[slot])
                dn2[rows,:]=dn2[rows,:]+(dot(dg[rows,:],wgb[slot],NT)+dot(du[rows,:],wub[slot],NT))
                return 0
            lax.fori_loop(0,3,back,0)
            @pl.when(c==3)
            def _(): N.rs(0,1)
            def wgrad(k,_):
                rr=pl.ds(pl.multiple_of(k*(Dm//2),Dm//2),Dm//2)
                M.g[0][slot,k,:,:,0:F]=dot(n2t[rr,:],dg[...]).reshape(RING,48,F).astype(BF)
                M.g[0][slot,k,:,:,F:2*F]=dot(n2t[rr,:],du[...]).reshape(RING,48,F).astype(BF)
                M.g[0][slot,k,:,:,2*F:3*F]=dot(ogt[rr,:],hid[...]).reshape(RING,48,F).astype(BF)
                return 0
            lax.fori_loop(0,2,wgrad,0)
            @pl.when(lax.rem(c,2)==0)
            def _(): M.start(c//2)
            @pl.when(lax.rem(c,2)==1)
            def _(): N.start(c//2)
            @pl.when(c==2)
            def _(): N.rs(0,0)
            return 0
        lax.fori_loop(0,4,step,0)
        gx[...]=jnp.zeros_like(gx)
        def post(i,gpart):
            rows=pl.ds(pl.multiple_of(i*W,W),W)
            r=res[rows,:]; d=dn2[rows,:]
            acc[rows,:]=acc[rows,:]+r
            i2=lax.rsqrt(jnp.mean(r*r,axis=1,keepdims=True)+EPS)
            s=gain_m[1:2]*d
            dr=og[rows,:].astype(F32)+i2*s-r*(i2*i2*i2)*jnp.mean(s*r,axis=1,keepdims=True)
            res[rows,:]=dr
            da=dr.astype(BF)
            n2[rows,:]=da
            dhs[rows,:]=dot(da,wop[...],NT).astype(BF)
            return gpart+jnp.sum(d*r*i2,axis=0,keepdims=True)
        gpart=lax.fori_loop(0,3,post,jnp.zeros((1,Dm),F32))
        c_dh.start()
        c_out=pltpu.make_async_copy(acc,out_h,lsem.at[10]); c_out.start()
        gx[0,1:2]=gpart
        N.rs(0,2); M.first(0)
        def own(i,_):
            rows=pl.ds(pl.multiple_of(i*W,W),W)
            n2t[:,rows]=n2[rows,:].T
            dh[pl.ds(pl.multiple_of(mine+i*W,W),W),:]=dot(n2[rows,:],wo[...],NT).astype(BF)
            return 0
        lax.fori_loop(0,3,own,0)
        def ograd(k,_):
            rr=pl.ds(pl.multiple_of(k*(Dm//2),Dm//2),Dm//2)
            O.g[0][0,k]=dot(n2t[rr,:],hrecv[...]).reshape(RING,48,H).astype(BF)
            O.g[0][1,k]=dot(n2t[rr,:],heads[pl.ds(mine,R),:]).reshape(RING,48,H).astype(BF)
            return 0
        lax.fori_loop(0,2,ograd,0)
        O.start(0); O.start(1)
        N.rs(0,3); N.xstart(0); N.first(1)
        c_out.wait()
    V=pltpu.VMEM
    pl.run_scoped(mlp,V((R,Dm),BF),V((Dm,R),BF),V((Dm,R),BF),V((R,Dm),F32),V((R,Dm),F32),V((R,F),BF),V((R,F),BF),V((R,F),BF),
                  V((2,Dm,F),BF),V((2,Dm,F),BF),V((2,F,Dm),BF))

    def attn(qe,ke,ve,cos_o,sin_o,nrm,x_p,wc,nt,doe,kt,dqt,ds_s,dn):
        ld=[pltpu.make_async_copy(s,d,lsem.at[i]) for i,(s,d) in enumerate(((norm_h,nrm),(ke_h,ke),(qe_h,qe),(ve_h,ve),(co_h,cos_o),(si_h,sin_o),(xp_h,x_p)))]
        ld+=[pltpu.make_async_copy(s.at[:,pl.ds(128*q,128)],wc.at[q,:,pl.ds(128*i,128)],lsem.at[12+3*q+i]) for q in range(nh//2) for i,s in enumerate((wq_h,wk_h,wv_h))]
        for q in ld: q.start()
        M.rs(0,0); O.push(0)
        ld[0].wait()
        def tr(i,_):
            c=pl.ds(pl.multiple_of(i*B,B),B)
            nt[:,c]=nrm[c,:].T
            return 0
        lax.fori_loop(0,nb,tr,0)
        N.rs(1,0); M.rs(0,1)
        for q in ld[1:]: q.wait()
        c_dh.wait(); N.rs(1,1)
        l=lanes((B,128)); low=l<64
        causal=lax.broadcasted_iota(jnp.int32,(B,B),0)<=lax.broadcasted_iota(jnp.int32,(B,B),1)
        def pair(p,_):
            cols=pl.ds(pl.multiple_of(p*128,128),128)
            for i in range(nb):
                rows=slice(i*B,(i+1)*B)
                d=dh[rows,cols].astype(F32); o=heads[rows,cols].astype(F32)
                t=d*o
                for hh in range(2):
                    if hh: t=pltpu.roll(t,64,1); d=pltpu.roll(d,64,1)
                    delta=jnp.sum(jnp.where(low,t,0.0),axis=1,keepdims=True)
                    a,b,c=split3(-delta)
                    doe[hh,rows,:]=jnp.where(low,d,jnp.where(l==64,a,jnp.where(l==65,b,jnp.where(l==66,c,0.0)))).astype(BF)
                    kt[hh,:,rows]=ke[2*p+hh,rows,:].T[0:64]
            dqt[...]=jnp.zeros_like(dqt)
            @pl.when(p==0)
            def _(): M.rs(0,2)
            @pl.when(p==2)
            def _(): M.ag(0,1)
            for j in range(nb):
                ks=slice(j*B,(j+1)*B); n0=j*B
                outs=[]
                for hh in range(2):
                    h=2*p+hh
                    s=dot(ke[h,ks,:],qe[h,n0:,:],NT)
                    dp=dot(ve[h,ks,:],doe[hh,n0:,:],NT)
                    sd=jnp.where(causal,s[:,:B],BIG)
                    s=sd if j==nb-1 else jnp.concatenate([sd,s[:,B:]],axis=1)
                    pt=jnp.exp2(s)
                    ds=(pt*dp).astype(BF)
                    pt=pt.astype(BF)
                    dv=dot(pt,doe[hh,n0:,:])
                    dk=dot(ds,qe[h,n0:,:])*LN2
                    dqt[64*hh:64*hh+64,n0:]+=dot(kt[hh,:,ks],ds)
                    outs.append((dk,dv))
                dk=jnp.where(low,outs[0][0],pltpu.roll(outs[1][0],64,1))
                dv=jnp.where(low,outs[0][1],pltpu.roll(outs[1][1],64,1))
                co=cos_o[ks,:]; si=sin_o[ks,:]
                ds_s[p,ks,128:256]=(dk*co-swap32(dk)*si).astype(BF)
                ds_s[p,ks,256:384]=dv.astype(BF)
                if j==0:
                    @pl.when(p==0)
                    def _(): N.rs(1,2)
                    @pl.when(p==1)
                    def _(): C.first(0); O.rs(0,0)
                    @pl.when(p==2)
                    def _(): C.first(1); C.rs(0,1); N.ag(0,1)
                if j==1:
                    @pl.when(p==0)
                    def _(): O.first(0)
                    @pl.when(p==1)
                    def _(): M.ag(0,0)
                    @pl.when(p==2)
                    def _(): O.rs(0,2)
                if j==3:
                    @pl.when(p==0)
                    def _(): M.rs(0,3); M.agstart(0)
                    @pl.when(p==1)
                    def _(): C.rs(0,0); N.ag(0,0)
                    @pl.when(p==2)
                    def _(): C.rs(1,0); M.ag(0,2)
            for i in range(nb):
                rows=slice(i*B,(i+1)*B)
                dq=dqt[:,rows].T*(HD**-0.5)
                co=cos_o[rows,:]; si=sin_o[rows,:]
                ds_s[p,rows,0:128]=(dq*co-swap32(dq)*si).astype(BF)
            for c in range(2):
                v=dot(nt[c*(Dm//2):(c+1)*(Dm//2),:],ds_s[p])
                C.g[0][p,c]=v.reshape(RING,Dm//16,384).astype(BF)
            C.start(p)
            @pl.when(p==0)
            def _(): N.rs(1,3); N.agstart(0)
            @pl.when(p==1)
            def _(): O.rs(0,1)
            @pl.when(p==2)
            def _(): C.rs(0,2); N.ag(0,2); O.rs(0,3); O.agstart(0)
            return 0
        lax.fori_loop(0,nh//2,pair,0)
        def c_dn(c): return copy_to(snd.at[blk(c)],rcv.at[blk(c)],sems,2+c,{"mp":1-mp})
        def part(r0,xr,c):
            rows=pl.ds(pl.multiple_of(r0,W),W)
            v=dot(ds_s[0,rows,:],wc[0],NT)+dot(ds_s[1,rows,:],wc[1],NT)+dot(ds_s[2,rows,:],wc[2],NT)
            x=xr[blk(c)].astype(F32)
            xr=x*lax.rsqrt(jnp.mean(x*x,axis=1,keepdims=True)+EPS)
            return v, jnp.sum(v*xr,axis=0,keepdims=True)
        gsum=jnp.zeros((1,Dm),F32)
        for c in range(3):
            v,gs=part(theirs+c*W,x_p,c); gsum=gsum+gs
            snd[blk(c)]=v.astype(BF); c_dn(c).start()
            if c==0: C.rs(0,3); C.agstart(0); C.rs(1,1); M.ag(0,3)
            if c==1: C.first(2); N.ag(0,3); O.ag(0,0)
            if c==2: C.rs(1,2)
        for c in range(3):
            v,gs=part(mine+c*W,x_ref,c); gsum=gsum+gs
            dn[blk(c)]=v
            if c==0: C.rs(2,0); C.ag(0,0)
            if c==1: C.rs(1,3); C.agstart(1); O.ag(0,1)
        gx[0,0:1]=gsum
        c_gc=copy_to(gx.at[0],gx.at[1],sems,6,{"core":1-at.core}); c_gc.start()
        C.rs(2,1); C.ag(0,1); O.ag(0,2)
        c_gc.wait(); gring[0]=gx[0]+gx[1]
        def c_gr(d,t): return copy_to(gring.at[0 if t==0 else 4*d+t],gring.at[4*d+t+1],sems,7+4*d+t,{"chip":at.nxt[d]})
        c_gr(0,0).start(); c_gr(1,0).start()
        gtot=gring[0]
        for t in range(4):
            for d in range(2):
                if t<4-d:
                    c_gr(d,t).wait()
                    if t+1<4-d: c_gr(d,t+1).start()
                    gtot=gtot+gring[4*d+t+1]
            if t==0: C.rs(2,2); C.ag(1,0); C.ag(0,2)
            if t==1: C.rs(2,3); C.agstart(2); C.ag(1,1); C.ag(0,3); O.ag(0,3)
            if t==2: C.ag(2,0); C.ag(1,2)
            if t==3: C.ag(2,1); C.ag(1,3)
        gx[2]=gtot
        c_gx=copy_to(gx.at[2],gx.at[3],sems,5,{"mp":1-mp}); c_gx.start()
        C.ag(2,2); C.ag(2,3)
        for c in range(3):
            c_dn(c).wait()
            r=blk(c)
            d=dn[r]+rcv[r].astype(F32)
            x=x_ref[r].astype(F32)
            i1=lax.rsqrt(jnp.mean(x*x,axis=1,keepdims=True)+EPS)
            s=gain_a[0:1]*d
            res[r]=res[r]+i1*s-x*(i1*i1*i1)*jnp.mean(s*x,axis=1,keepdims=True)
        c_gx.wait(); gains_out[...]=gx[2]+gx[3]
        c_ig=pltpu.make_async_copy(res,ig_h,lsem.at[11]); c_ig.start()
        M.finish(0); N.finish(0); O.finish(0)
        for v in range(3): C.finish(v)
        c_ig.wait()
    hT=V((nh,T,128),BF)
    pl.run_scoped(attn,hT,hT,hT,V((T,128),F32),V((T,128),F32),V((T,Dm),BF),V((R,Dm),BF),V((nh//2,Dm,H),BF),
                  V((Dm,T),BF),V((2,T,128),BF),V((2,64,T),BF),V((128,T),F32),V((nh//2,T,H),BF),V((R,Dm),F32))

def main_call(x,og,heads,hrecv,wo,wop,gain_a,gain_m,hbm,cid):
    R,Dm=x.shape; T,H=heads.shape
    Vs=pl.BlockSpec(memory_space=pltpu.VMEM); N=pl.BlockSpec(memory_space=pl.ANY); sd=jax.ShapeDtypeStruct; V=pltpu.VMEM
    scs=[s.scratch() for s in (RING_M,RING_N,RING_O,RING_C)]
    local=[V((R,H),BF),V((T,H),BF),V((R,Dm),F32)]+[V((R,Dm),BF)]*2
    local+=[V((4,8,Dm),F32),V((RING,8,Dm),F32),pltpu.SemaphoreType.DMA((2,7+RING)),pltpu.SemaphoreType.DMA((21,)),pltpu.SemaphoreType.DMA((2,3))]
    outs=[sd((R,Dm),F32)]*2+[sd((2,2,RING,48,1536),BF),sd((2,RING,48,H),BF),sd((3,2,RING,48,384),BF),sd((8,Dm),F32)]
    return pl.pallas_call(functools.partial(main_kernel,*[len(s) for s in scs]),
        out_shape=tuple(outs), in_specs=[Vs]*8+[N]*len(hbm), out_specs=(N,)*5+(Vs,),
        scratch_shapes=sum(scs,[])+local,
        compiler_params=pltpu.CompilerParams(collective_id=cid,has_side_effects=True,vmem_limit_bytes=67043328),
        name="mlp_and_backward")(x,og,heads,hrecv,wo,wop,gain_a,gain_m,*hbm)

def widen_kernel(mlp,wo,qkv,gate,up,down,out,query,key,value):
    F=mlp.shape[2]//3; H=wo.shape[1]; B=mlp.shape[1]
    for q in range(2):
        cs=slice(F*q,F*q+F)
        gate[:,cs]=mlp[q,:,0:F].astype(F32)
        up[:,cs]=mlp[q,:,F:2*F].astype(F32)
        down[cs,:]=mlp[q,:,2*F:3*F].astype(F32).T
    out[...]=wo[...].astype(F32).T
    for p in range(qkv.shape[0]):
        cs=slice(128*p,128*p+128)
        query[:,cs]=qkv[p,:,0:128].astype(F32)
        key[:,cs]=qkv[p,:,128:256].astype(F32)
        value[:,cs]=qkv[p,:,256:384].astype(F32)

def widen(mlp,wo,qkv):
    Dm,H=wo.shape; F=mlp.shape[2]//3; B=128; P3=qkv.shape[0]
    sd=jax.ShapeDtypeStruct
    row=lambda n: pl.BlockSpec((B,n),lambda i:(i,0))
    col=lambda n: pl.BlockSpec((n,B),lambda i:(0,i))
    return pl.pallas_call(widen_kernel,grid=(Dm//B,),
        out_shape=(sd((Dm,2*F),F32),sd((Dm,2*F),F32),sd((2*F,Dm),F32),sd((H,Dm),F32))+(sd((Dm,H),F32),)*3,
        in_specs=[pl.BlockSpec((2,B,3*F),lambda i:(0,i,0)),row(H),pl.BlockSpec((P3,B,H),lambda i:(0,i,0))],
        out_specs=(row(2*F),row(2*F),col(2*F),col(H),row(H),row(H),row(H)),
        compiler_params=pltpu.CompilerParams(vmem_limit_bytes=48*2**20),name="widen")(mlp,wo,qkv)


def on_device(layer_input, gain_attn, w_query, w_key, w_value, w_out, gain_mlp, w_gate, w_up, w_down,
              segment_start, segment_parent, out_grad):
    weights = (w_out, w_gate, w_up, w_down)
    gains = jnp.stack([gain_attn, gain_mlp]).astype(F32)
    x_peer, normed, cosine, sine, ke, ve, qe, heads, heads_peer, peer_out, peer_gate, peer_up, peer_down = front(
        layer_input, gains, w_query, w_key, w_value, segment_start, segment_parent, weights, 2
    )
    output, input_grad, mlp_g, out_g, qkv_g, gain_g = main_call(
        layer_input, out_grad, heads, heads_peer, w_out, peer_out, gains, gains,
        (w_gate, w_up, w_down, peer_gate, peer_up, peer_down, qe, ke, ve, cosine, sine, normed, x_peer,
         w_query, w_key, w_value), 1,
    )
    sums = [mlp_g.reshape(2, -1, mlp_g.shape[-1]), out_g.reshape(-1, out_g.shape[-1]), qkv_g.reshape(3, -1, qkv_g.shape[-1]), gain_g]
    if lax.axis_size("grp") > 1:
        sums = lax.psum([s.astype(F32) for s in sums], "grp")
    mlp_g, out_g, qkv_g, gain_g = sums
    gate_g, up_g, down_g, out_g, query_g, key_g, value_g = widen(mlp_g, out_g, qkv_g)
    return (
        output, input_grad, gain_g[0], query_g, key_g, value_g, out_g, gain_g[1], gate_g, up_g, down_g,
    )


def solution(mesh):
    fine = Mesh(mesh.devices.reshape(-1, RING, 2, mesh.shape["mp"]), ("grp", "chip", "core", "mp"))
    dp = ("grp", "chip", "core")
    tok, col, row, tree = P(dp + ("mp",), None), P(None, "mp"), P("mp", None), P(dp, None)
    in_specs = (tok, P(), col, col, col, row, P(), col, col, row, tree, tree, tok)
    out_specs = (tok, tok, P(), col, col, col, row, P(), col, col, row)
    return jax.shard_map(on_device, mesh=fine, in_specs=in_specs, out_specs=out_specs, check_vma=False)
```

profile of v0, /device:TPU:0, one launch (start us, length us, event | category | flops | bytes accessed | tf_op | source)
XLA Modules:
  0.0 230.2 jit_solution(2194223759924476605)
XLA Ops:
  0.6 0.7 stack.9
  1.3 0.7 stack.10
  2.0 0.6 maximum_convert_fusion.gain.refs_6_.refs_7_
  2.6 68.8 %attention_forward.1 = (bf16[768,768]{1,0:T(8,128)(2,1)}, bf16[1536,768]{1,0:T(8,128)(2,1)}, f32[1536,128]{1,0:T(8,128)}, f32[1536,128]{1,0:T(8,128)}, bf16[6,15...) custom-call(s32[1,7]{1,0:T(1,128)} %starts.1, ...), custom_call_target="tpu_custom_call" | custom-call | tf_op jit(solution)/shard_map/attention_forward/pallas_call | solution.py:224
  71.4 142.8 %mlp_and_backward.1 = (f32[768,768]{1,0:T(8,128)}, f32[768,768]{1,0:T(8,128)}, bf16[2,2,8,48,1536]{4,3,2,1,0:T(8,128)(2,1)}, bf16[2,8,48,384]{3,2,1,0:T(8,128)(2...) custom-call(bf16[768,768]{1,0:T(8,128)(2,1)} %refs_0_.3, bf16[768,768]{1,0:T(8,128)(2,1)} %refs_1_.3, ...), custom_call_target="tpu_custom_call" | custom-call | tf_op jit(solution)/shard_map/mlp_and_backward/pallas_call | solution.py:631
  214.2 1.4 slice_reduce_fusion
  215.6 0.0 copy-start
  215.6 1.5 copy-done
  217.1 0.0 copy-start.1
  217.1 1.1 copy-done.1
  218.2 0.0 copy-start.3
  218.2 8.0 %widen.1 = (f32[768,1024]{1,0:T(8,128)}, f32[768,1024]{1,0:T(8,128)}, f32[1024,768]{1,0:T(8,128)}, f32[384,768]{1,0:T(8,128)}, f32[768,384]{1,0:T(8,128)}, /*index=5*/f32[768,384]{1,0:T(8,128)}, f32[768,384]{1,0:T(8,128)}) custom-call(bf16[2,768,1536]{2,1,0:T(8,128)(2,1)} %bitcast.5, bf16[768,384]{1,0:T(8,128)(2,1)S(1)} %bitcast.4, ...), custom_call_target="tpu_custom_call" | custom-call | tf_op jit(solution)/shard_map/widen/pallas_call | solution.py:656
  226.2 0.0 copy-done.3
  226.2 0.0 copy-start.2
  226.2 1.4 copy.26
  227.6 1.1 copy-done.2
  228.7 1.4 copy.27
Async XLA Ops:
  215.6 1.5 copy-start
  217.1 1.1 copy-start.1
  218.2 8.0 %copy-start.3 = (f32[768,768]{1,0:T(8,128)S(1)}, f32[768,768]{1,0:T(8,128)}, u32[]{:S(2)}) copy-start(f32[768,768]{1,0:T(8,128)} %get-tuple-element.76) | copy-start | bytes 7077892
  226.2 2.5 %copy-start.2 = (f32[768,768]{1,0:T(8,128)S(1)}, f32[768,768]{1,0:T(8,128)}, u32[]{:S(2)}) copy-start(f32[768,768]{1,0:T(8,128)} %get-tuple-element.77) | copy-start | bytes 7077892
where the time goes:
time: 231 us; the launch traced here: 230 us
  Pallas kernels  220 us (95%)
  local copies, waits for them, and re-layouts  9.26 us (4%)
    pallas_call x1, Pallas kernels, main_call(): pl.pallas_call(functools.partial(main_kernel, *[len(s) for s in scs]), ou...  143 us
    pallas_call x1, Pallas kernels, front(): pl.pallas_call(functools.partial(front_kernel, nseg), out_shape=(sd((R, D...  68.8 us
    pallas_call x1, Pallas kernels, widen(): pl.pallas_call(widen_kernel, grid=(Dm // B,), out_shape=(sd((Dm, 2 * F),...  8.04 us
    unnamed x10, local copies, waits for them, and re-layouts  6.46 us

commit v1 on v0

--- a/solution.py
+++ b/solution.py
@@ -82,7 +82,7 @@
         b=pltpu.get_barrier_semaphore()
         ds=[{"core":1-self.core},{"mp":1-self.mp},{"chip":self.nxt[0]},{"chip":self.nxt[1]}]
         for d in ds: pl.semaphore_signal(b, inc=1, device_id=d, device_id_type=MESH)
-        pl.semaphore_wait(b, len(ds))
+        return lambda: pl.semaphore_wait(b, len(ds))
 
 def copy_to(src,dst,sems,k,dev):
     return pltpu.make_async_remote_copy(src,dst,sems.at[0,k],sems.at[1,k],device_id=dev,device_id_type=MESH)
@@ -134,7 +134,7 @@
     R=x_ref.shape[0]; T=2*R; B=256; nh=wq.shape[1]//HD
     G=Gather(at,src,out,[a%2 for a in range(NW)],wsems)
     mine=pl.multiple_of(mp*R,R); theirs=pl.multiple_of((1-mp)*R,R)
-    at.barrier()
+    at.barrier()()
     peer={"mp":1-mp}
     NG=NW
     for a in range(NG): G.cx(a).start()
@@ -154,7 +154,7 @@
             rows=pl.ds(pl.multiple_of(base+c*B,B),B)
             x=xr[pl.ds(pl.multiple_of(c*B,B),B),:].astype(F32)
             r1=lax.rsqrt(jnp.mean(x*x,axis=1,keepdims=True)+EPS)
-            n=(x*r1*gain[0:1]).astype(BF)
+            n=(x*r1*gain[...].astype(F32).reshape(1,-1)).astype(BF)
             normed[rows,:]=n
             co=cos_o[rows,:]; si=sin_o[rows,:]; qf=qf_s[rows,:].astype(F32); kf=kf_s[rows,:].astype(F32)
             qq=dot(n,wq[...]); kk=dot(n,wk[...]); vv=dot(n,wv[...])
@@ -181,9 +181,10 @@
     for a in range(NG): G.ag(a,2)
     def put_q(p): return pltpu.make_async_copy(qe.at[pl.ds(2*p,2)],big[6].at[pl.ds(2*p,2)],osem.at[6+p])
     causal=lax.broadcasted_iota(jnp.int32,(B,B),1)<=lax.broadcasted_iota(jnp.int32,(B,B),0)
-    def c_h(p):
+    NB=R//B
+    def c_h(p,q):
         cs=pl.ds(pl.multiple_of(p*128,128),128)
-        return pltpu.make_async_remote_copy(heads.at[pl.ds(theirs,R),cs],hrecv.at[:,cs],sems.at[0,1+p],sems.at[1,1+p],device_id=peer,device_id_type=MESH)
+        return pltpu.make_async_remote_copy(heads.at[pl.ds(pl.multiple_of(theirs+q*B,B),B),cs],hrecv.at[pl.ds(q*B,B),cs],sems.at[0,1+NB*p+q],sems.at[1,1+NB*p+q],device_id=peer,device_id_type=MESH)
     def attend(p,_):
         cs=pl.ds(pl.multiple_of(p*128,128),128)
         for i in range(T//B):
@@ -204,18 +205,20 @@
                 qe[h,rows,:]=jnp.where(lb==72,a,jnp.where(lb==73,b,jnp.where(lb==74,c,q.astype(F32)))).astype(BF)
                 outs.append(o)
             heads[rows,cs]=jnp.where(low,outs[0],pltpu.roll(outs[1],64,1)).astype(BF)
+            @pl.when(1-mp==i//NB)
+            def _(): c_h(p,i%NB).start()
             if i==3:
-                @pl.when(p==1)
+                @pl.when(p==2)
                 def _():
                     for a in range(NG): G.ag(a,3)
-        c_h(p).start()
         put_q(p).start()
         return 0
     lax.fori_loop(0,nh//2,attend,0)
     for a in range(NW): G.finish(a)
     for q in puts: q.wait()
     for p in range(nh//2): put_q(p).wait()
-    for p in range(nh//2): c_h(p).wait()
+    for p in range(nh//2):
+        for q in range(NB): c_h(p,q).wait()
 
 def front(x,gain,wq,wk,wv,starts,parents,weights,cid):
     R,Dm=x.shape; T=2*R; H=wq.shape[1]; nh=H//HD; nseg=starts.shape[1]; NW=len(weights)
@@ -225,7 +228,7 @@
         out_shape=(sd((R,Dm),BF),sd((T,Dm),BF),sd((T,128),F32),sd((T,128),F32),hT,hT,hT,sd((T,H),BF),sd((R,H),BF))+tuple(sd(w.shape,BF) for w in weights),
         in_specs=[S,S]+[Vs]*5+[N]*NW, out_specs=(N,)*7+(Vs,)*2+(N,)*NW,
         scratch_shapes=[V((R,Dm),BF),V((T,Dm),BF),V((T,128),F32),V((T,128),F32),V((nh,T,128),BF),V((nh,T,128),BF),V((nh,T,128),BF),V((T,128),BF),V((T,128),BF),
-            pltpu.SemaphoreType.DMA((2,1+nh//2)),pltpu.SemaphoreType.DMA((2,NW,18)),pltpu.SemaphoreType.DMA((6+nh//2,))],
+            pltpu.SemaphoreType.DMA((2,1+(nh//2)*(R//256))),pltpu.SemaphoreType.DMA((2,NW,18)),pltpu.SemaphoreType.DMA((6+nh//2,))],
         compiler_params=pltpu.CompilerParams(collective_id=cid,has_side_effects=True,vmem_limit_bytes=67043328),
         name="attention_forward")(starts,parents,x,gain,wq,wk,wv,*weights)
 
@@ -351,6 +354,38 @@
 RING_N=Ring(SHAPES_M,KINDS_M,2,0,[(1,0)],False,lambda u: 1)
 RING_O=Ring([(48,384)],[[(0,256,0),(256,128,1)]],2,2,[(1,0)])
 RING_C=Ring([(48,384)],[[(0,256,0),(256,128,1)]],3,3,[])
+SCHEDULE={
+"m1":[("N","rs",0,2),("M","first",0)],
+"m2":[("N","rs",0,3),("N","xstart",0),("N","first",1)],
+"a0":[("M","rs",0,0),("O","push",0)],
+"a1":[("N","rs",1,0),("M","rs",0,1)],
+"a2":[("N","rs",1,1)],
+"p0s":[("M","rs",0,2)],
+"p0j0":[("N","rs",1,2)],
+"p0j1":[("O","first",0)],
+"p0j3":[("M","rs",0,3),("M","agstart",0)],
+"p0e":[("N","rs",1,3),("N","agstart",0)],
+"p1j0":[("C","first",0),("O","rs",0,0)],
+"p1j1":[("M","ag",0,0)],
+"p1j3":[("C","rs",0,0),("N","ag",0,0)],
+"p1e":[("O","rs",0,1)],
+"p2s":[("M","ag",0,1)],
+"p2j0":[("C","first",1),("C","rs",0,1),("N","ag",0,1)],
+"p2j1":[("O","rs",0,2)],
+"p2j3":[("C","rs",1,0),("M","ag",0,2)],
+"p2e":[("C","rs",0,2),("N","ag",0,2),("O","rs",0,3),("O","agstart",0)],
+"t0":[("C","rs",0,3),("C","agstart",0),("C","rs",1,1),("M","ag",0,3)],
+"t1":[("C","first",2),("N","ag",0,3),("O","ag",0,0)],
+"t2":[("C","rs",1,2)],
+"u0":[("C","rs",2,0),("C","ag",0,0)],
+"u1":[("C","rs",1,3),("C","agstart",1),("O","ag",0,1)],
+"g":[("C","rs",2,1),("C","ag",0,1),("O","ag",0,2)],
+"g0":[("C","rs",2,2),("C","ag",1,0),("C","ag",0,2)],
+"g1":[("C","rs",2,3),("C","agstart",2),("C","ag",1,1),("C","ag",0,3),("O","ag",0,3)],
+"g2":[("C","ag",2,0),("C","ag",1,2)],
+"g3":[("C","ag",2,1),("C","ag",1,3)],
+"z":[("C","ag",2,2),("C","ag",2,3)],
+}
 def main_kernel(nM,nN,nO,nC,*refs):
     refs=list(refs)
     def take(n):
@@ -363,13 +398,17 @@
     at=Place(); mp=at.mp
     R,Dm=x_ref.shape; T=2*R; nh=qe_h.shape[0]; B=256; nb=T//B; H=wo.shape[0]; F=512
     core=at.core
+    rings={}
+    def tick(site):
+        for name,op,*args in SCHEDULE.get(site,()): getattr(rings[name],op)(*args)
     def dst_m(q): return lambda v,a,ch: outM[0].at[q,core,ch]
     def dst_c(v,a,ch): return outC[0].at[v,core,ch]
     M=RING_M.bind(at,dst_m(0),scM); N=RING_N.bind(at,dst_m(1),scN,M.g); O=RING_O.bind(at,lambda v,a,ch: outO[0].at[core,ch],scO); C=RING_C.bind(at,dst_c,scC)
+    rings.update(M=M,N=N,O=O,C=C)
     mine=pl.multiple_of(mp*R,R); theirs=pl.multiple_of((1-mp)*R,R)
     W=R//3
     def blk(i): return pl.ds(i*W,W)
-    at.barrier()
+    arrived=at.barrier()
     c_dh=copy_to(dhs,dh.at[pl.ds(mine,R)],sems,0,{"mp":1-mp})
 
     def mlp(n2,n2t,ogt,acc,dn2,hid,dg,du,wgb,wub,wdb):
@@ -383,12 +422,13 @@
             rows=pl.ds(pl.multiple_of(i*W,W),W); mr=pl.ds(pl.multiple_of(mine+i*W,W),W)
             r=x_ref[rows,:].astype(F32)+dot(heads[mr,:],wo[...])+dot(hrecv[rows,:],wop[...])
             res[rows,:]=r
-            n=(r*lax.rsqrt(jnp.mean(r*r,axis=1,keepdims=True)+EPS)*gain_m[1:2]).astype(BF)
+            n=(r*lax.rsqrt(jnp.mean(r*r,axis=1,keepdims=True)+EPS)*gain_m[...].astype(F32).reshape(1,-1)).astype(BF)
             n2[rows,:]=n
             n2t[:,rows]=n.T
             ogt[:,rows]=og[rows,:].T
             return 0
         lax.fori_loop(0,3,pre,0)
+        arrived()
         acc[...]=jnp.zeros_like(acc); dn2[...]=jnp.zeros_like(dn2)
         def step(c,_):
             slot=lax.rem(c,2)
@@ -436,13 +476,14 @@
             def _(): N.rs(0,0)
             return 0
         lax.fori_loop(0,4,step,0)
+        tick("m0")
         gx[...]=jnp.zeros_like(gx)
         def post(i,gpart):
             rows=pl.ds(pl.multiple_of(i*W,W),W)
             r=res[rows,:]; d=dn2[rows,:]
             acc[rows,:]=acc[rows,:]+r
             i2=lax.rsqrt(jnp.mean(r*r,axis=1,keepdims=True)+EPS)
-            s=gain_m[1:2]*d
+            s=gain_m[...].astype(F32).reshape(1,-1)*d
             dr=og[rows,:].astype(F32)+i2*s-r*(i2*i2*i2)*jnp.mean(s*r,axis=1,keepdims=True)
             res[rows,:]=dr
             da=dr.astype(BF)
@@ -453,7 +494,7 @@
         c_dh.start()
         c_out=pltpu.make_async_copy(acc,out_h,lsem.at[10]); c_out.start()
         gx[0,1:2]=gpart
-        N.rs(0,2); M.first(0)
+        tick("m1")
         def own(i,_):
             rows=pl.ds(pl.multiple_of(i*W,W),W)
             n2t[:,rows]=n2[rows,:].T
@@ -467,7 +508,7 @@
             return 0
         lax.fori_loop(0,2,ograd,0)
         O.start(0); O.start(1)
-        N.rs(0,3); N.xstart(0); N.first(1)
+        tick("m2")
         c_out.wait()
     V=pltpu.VMEM
     pl.run_scoped(mlp,V((R,Dm),BF),V((Dm,R),BF),V((Dm,R),BF),V((R,Dm),F32),V((R,Dm),F32),V((R,F),BF),V((R,F),BF),V((R,F),BF),
@@ -477,16 +518,16 @@
         ld=[pltpu.make_async_copy(s,d,lsem.at[i]) for i,(s,d) in enumerate(((norm_h,nrm),(ke_h,ke),(qe_h,qe),(ve_h,ve),(co_h,cos_o),(si_h,sin_o),(xp_h,x_p)))]
         ld+=[pltpu.make_async_copy(s.at[:,pl.ds(128*q,128)],wc.at[q,:,pl.ds(128*i,128)],lsem.at[12+3*q+i]) for q in range(nh//2) for i,s in enumerate((wq_h,wk_h,wv_h))]
         for q in ld: q.start()
-        M.rs(0,0); O.push(0)
+        tick("a0")
         ld[0].wait()
         def tr(i,_):
             c=pl.ds(pl.multiple_of(i*B,B),B)
             nt[:,c]=nrm[c,:].T
             return 0
         lax.fori_loop(0,nb,tr,0)
-        N.rs(1,0); M.rs(0,1)
+        tick("a1")
         for q in ld[1:]: q.wait()
-        c_dh.wait(); N.rs(1,1)
+        c_dh.wait(); tick("a2")
         l=lanes((B,128)); low=l<64
         causal=lax.broadcasted_iota(jnp.int32,(B,B),0)<=lax.broadcasted_iota(jnp.int32,(B,B),1)
         def pair(p,_):
@@ -502,10 +543,10 @@
                     doe[hh,rows,:]=jnp.where(low,d,jnp.where(l==64,a,jnp.where(l==65,b,jnp.where(l==66,c,0.0)))).astype(BF)
                     kt[hh,:,rows]=ke[2*p+hh,rows,:].T[0:64]
             dqt[...]=jnp.zeros_like(dqt)
-            @pl.when(p==0)
-            def _(): M.rs(0,2)
-            @pl.when(p==2)
-            def _(): M.ag(0,1)
+            for q in range(3):
+                if "p%ds"%q in SCHEDULE:
+                    @pl.when(p==q)
+                    def _(): tick("p%ds"%q)
             for j in range(nb):
                 ks=slice(j*B,(j+1)*B); n0=j*B
                 outs=[]
@@ -527,27 +568,10 @@
                 co=cos_o[ks,:]; si=sin_o[ks,:]
                 ds_s[p,ks,128:256]=(dk*co-swap32(dk)*si).astype(BF)
                 ds_s[p,ks,256:384]=dv.astype(BF)
-                if j==0:
-                    @pl.when(p==0)
-                    def _(): N.rs(1,2)
-                    @pl.when(p==1)
-                    def _(): C.first(0); O.rs(0,0)
-                    @pl.when(p==2)
-                    def _(): C.first(1); C.rs(0,1); N.ag(0,1)
-                if j==1:
-                    @pl.when(p==0)
-                    def _(): O.first(0)
-                    @pl.when(p==1)
-                    def _(): M.ag(0,0)
-                    @pl.when(p==2)
-                    def _(): O.rs(0,2)
-                if j==3:
-                    @pl.when(p==0)
-                    def _(): M.rs(0,3); M.agstart(0)
-                    @pl.when(p==1)
-                    def _(): C.rs(0,0); N.ag(0,0)
-                    @pl.when(p==2)
-                    def _(): C.rs(1,0); M.ag(0,2)
+                for q in range(3):
+                    if "p%dj%d"%(q,j) in SCHEDULE:
+                        @pl.when(p==q)
+                        def _(): tick("p%dj%d"%(q,j))
             for i in range(nb):
                 rows=slice(i*B,(i+1)*B)
                 dq=dqt[:,rows].T*(HD**-0.5)
@@ -557,12 +581,10 @@
                 v=dot(nt[c*(Dm//2):(c+1)*(Dm//2),:],ds_s[p])
                 C.g[0][p,c]=v.reshape(RING,Dm//16,384).astype(BF)
             C.start(p)
-            @pl.when(p==0)
-            def _(): N.rs(1,3); N.agstart(0)
-            @pl.when(p==1)
-            def _(): O.rs(0,1)
-            @pl.when(p==2)
-            def _(): C.rs(0,2); N.ag(0,2); O.rs(0,3); O.agstart(0)
+            for q in range(3):
+                if "p%de"%q in SCHEDULE:
+                    @pl.when(p==q)
+                    def _(): tick("p%de"%q)
             return 0
         lax.fori_loop(0,nh//2,pair,0)
         def c_dn(c): return copy_to(snd.at[blk(c)],rcv.at[blk(c)],sems,2+c,{"mp":1-mp})
@@ -576,17 +598,14 @@
         for c in range(3):
             v,gs=part(theirs+c*W,x_p,c); gsum=gsum+gs
             snd[blk(c)]=v.astype(BF); c_dn(c).start()
-            if c==0: C.rs(0,3); C.agstart(0); C.rs(1,1); M.ag(0,3)
-            if c==1: C.first(2); N.ag(0,3); O.ag(0,0)
-            if c==2: C.rs(1,2)
+            tick("t%d"%c)
         for c in range(3):
             v,gs=part(mine+c*W,x_ref,c); gsum=gsum+gs
             dn[blk(c)]=v
-            if c==0: C.rs(2,0); C.ag(0,0)
-            if c==1: C.rs(1,3); C.agstart(1); O.ag(0,1)
+            tick("u%d"%c)
         gx[0,0:1]=gsum
         c_gc=copy_to(gx.at[0],gx.at[1],sems,6,{"core":1-at.core}); c_gc.start()
-        C.rs(2,1); C.ag(0,1); O.ag(0,2)
+        tick("g")
         c_gc.wait(); gring[0]=gx[0]+gx[1]
         def c_gr(d,t): return copy_to(gring.at[0 if t==0 else 4*d+t],gring.at[4*d+t+1],sems,7+4*d+t,{"chip":at.nxt[d]})
         c_gr(0,0).start(); c_gr(1,0).start()
@@ -597,20 +616,17 @@
                     c_gr(d,t).wait()
                     if t+1<4-d: c_gr(d,t+1).start()
                     gtot=gtot+gring[4*d+t+1]
-            if t==0: C.rs(2,2); C.ag(1,0); C.ag(0,2)
-            if t==1: C.rs(2,3); C.agstart(2); C.ag(1,1); C.ag(0,3); O.ag(0,3)
-            if t==2: C.ag(2,0); C.ag(1,2)
-            if t==3: C.ag(2,1); C.ag(1,3)
+            tick("g%d"%t)
         gx[2]=gtot
         c_gx=copy_to(gx.at[2],gx.at[3],sems,5,{"mp":1-mp}); c_gx.start()
-        C.ag(2,2); C.ag(2,3)
+        tick("z")
         for c in range(3):
             c_dn(c).wait()
             r=blk(c)
             d=dn[r]+rcv[r].astype(F32)
             x=x_ref[r].astype(F32)
             i1=lax.rsqrt(jnp.mean(x*x,axis=1,keepdims=True)+EPS)
-            s=gain_a[0:1]*d
+            s=gain_a[...].astype(F32).reshape(1,-1)*d
             res[r]=res[r]+i1*s-x*(i1*i1*i1)*jnp.mean(s*x,axis=1,keepdims=True)
         c_gx.wait(); gains_out[...]=gx[2]+gx[3]
         c_ig=pltpu.make_async_copy(res,ig_h,lsem.at[11]); c_ig.start()
@@ -634,7 +650,9 @@
         compiler_params=pltpu.CompilerParams(collective_id=cid,has_side_effects=True,vmem_limit_bytes=67043328),
         name="mlp_and_backward")(x,og,heads,hrecv,wo,wop,gain_a,gain_m,*hbm)
 
-def widen_kernel(mlp,wo,qkv,gate,up,down,out,query,key,value):
+def widen_kernel(mlp,wo,qkv,y,dx,gains,gate,up,down,out,query,key,value,y_out,dx_out,ga,gm):
+    ga[...]=gains[0]; gm[...]=gains[1]
+    y_out[...]=y[...]; dx_out[...]=dx[...]
     F=mlp.shape[2]//3; H=wo.shape[1]; B=mlp.shape[1]
     for q in range(2):
         cs=slice(F*q,F*q+F)
@@ -648,27 +666,27 @@
         key[:,cs]=qkv[p,:,128:256].astype(F32)
         value[:,cs]=qkv[p,:,256:384].astype(F32)
 
-def widen(mlp,wo,qkv):
+def widen(mlp,wo,qkv,y,dx,gains):
     Dm,H=wo.shape; F=mlp.shape[2]//3; B=128; P3=qkv.shape[0]
     sd=jax.ShapeDtypeStruct
     row=lambda n: pl.BlockSpec((B,n),lambda i:(i,0))
+    rows_spec=pl.BlockSpec((y.shape[0]//(Dm//B),y.shape[1]),lambda i:(i,0))
     col=lambda n: pl.BlockSpec((n,B),lambda i:(0,i))
     return pl.pallas_call(widen_kernel,grid=(Dm//B,),
-        out_shape=(sd((Dm,2*F),F32),sd((Dm,2*F),F32),sd((2*F,Dm),F32),sd((H,Dm),F32))+(sd((Dm,H),F32),)*3,
-        in_specs=[pl.BlockSpec((2,B,3*F),lambda i:(0,i,0)),row(H),pl.BlockSpec((P3,B,H),lambda i:(0,i,0))],
-        out_specs=(row(2*F),row(2*F),col(2*F),col(H),row(H),row(H),row(H)),
-        compiler_params=pltpu.CompilerParams(vmem_limit_bytes=48*2**20),name="widen")(mlp,wo,qkv)
+        out_shape=(sd((Dm,2*F),F32),sd((Dm,2*F),F32),sd((2*F,Dm),F32),sd((H,Dm),F32))+(sd((Dm,H),F32),)*3+(sd(y.shape,F32),)*2+(sd((Dm,),F32),)*2,
+        in_specs=[pl.BlockSpec((2,B,3*F),lambda i:(0,i,0)),row(H),pl.BlockSpec((P3,B,H),lambda i:(0,i,0)),rows_spec,rows_spec,pl.BlockSpec((8,Dm),lambda i:(0,0))],
+        out_specs=(row(2*F),row(2*F),col(2*F),col(H),row(H),row(H),row(H),rows_spec,rows_spec)+(pl.BlockSpec((Dm,),lambda i:(0,)),)*2,
+        compiler_params=pltpu.CompilerParams(vmem_limit_bytes=67043328),name="widen")(mlp,wo,qkv,y,dx,gains)
 
 
 def on_device(layer_input, gain_attn, w_query, w_key, w_value, w_out, gain_mlp, w_gate, w_up, w_down,
               segment_start, segment_parent, out_grad):
     weights = (w_out, w_gate, w_up, w_down)
-    gains = jnp.stack([gain_attn, gain_mlp]).astype(F32)
     x_peer, normed, cosine, sine, ke, ve, qe, heads, heads_peer, peer_out, peer_gate, peer_up, peer_down = front(
-        layer_input, gains, w_query, w_key, w_value, segment_start, segment_parent, weights, 2
+        layer_input, gain_attn, w_query, w_key, w_value, segment_start, segment_parent, weights, 2
     )
     output, input_grad, mlp_g, out_g, qkv_g, gain_g = main_call(
-        layer_input, out_grad, heads, heads_peer, w_out, peer_out, gains, gains,
+        layer_input, out_grad, heads, heads_peer, w_out, peer_out, gain_attn, gain_mlp,
         (w_gate, w_up, w_down, peer_gate, peer_up, peer_down, qe, ke, ve, cosine, sine, normed, x_peer,
          w_query, w_key, w_value), 1,
     )
@@ -676,9 +694,11 @@
     if lax.axis_size("grp") > 1:
         sums = lax.psum([s.astype(F32) for s in sums], "grp")
     mlp_g, out_g, qkv_g, gain_g = sums
-    gate_g, up_g, down_g, out_g, query_g, key_g, value_g = widen(mlp_g, out_g, qkv_g)
+    gate_g, up_g, down_g, out_g, query_g, key_g, value_g, output, input_grad, gain_attn_grad, gain_mlp_grad = widen(
+        mlp_g, out_g, qkv_g, output, input_grad, gain_g
+    )
     return (
-        output, input_grad, gain_g[0], query_g, key_g, value_g, out_g, gain_g[1], gate_g, up_g, down_g,
+        output, input_grad, gain_attn_grad, query_g, key_g, value_g, out_g, gain_mlp_grad, gate_g, up_g, down_g,
     )
 
 

time: 231 us -> 224 us (0.970)
  local copies, waits for them, and re-layouts: 9.26 us -> 0 us
    unnamed x10 -> x0, local copies, waits for them, and re-layouts: 6.46 us -> none
    pallas_call x1, Pallas kernels: 8.04 us -> 11.3 us  [widen(): pl.pallas_call(widen_kernel, grid=(Dm // B,), out_shape=(sd((Dm, 2 * F),...]
where the time goes in v1:
time: 224 us; the launch traced here: 223 us
  Pallas kernels  222 us (99%)
    pallas_call x1, Pallas kernels, main_call(): pl.pallas_call(functools.partial(main_kernel, *[len(s) for s in scs]), ou...  142 us
    pallas_call x1, Pallas kernels, front(): pl.pallas_call(functools.partial(front_kernel, nseg), out_shape=(sd((R, D...  68.7 us
    pallas_call x1, Pallas kernels, widen(): pl.pallas_call(widen_kernel, grid=(Dm // B,), out_shape=(sd((Dm, 2 * F),...  11.3 us

profile of v1, /device:TPU:0, one launch (start us, length us, event | category | flops | bytes accessed | tf_op | source)
XLA Modules:
  0.0 223.3 jit_solution(547185276583123665)
XLA Ops:
  0.6 68.7 %attention_forward.1 = (bf16[768,768]{1,0:T(8,128)(2,1)}, bf16[1536,768]{1,0:T(8,128)(2,1)}, f32[1536,128]{1,0:T(8,128)}, f32[1536,128]{1,0:T(8,128)}, bf16[6,15...) custom-call(s32[1,7]{1,0:T(1,128)} %starts.1, ...), custom_call_target="tpu_custom_call" | custom-call | tf_op jit(solution)/shard_map/attention_forward/pallas_call | solution.py:227
  69.4 142.5 %mlp_and_backward.1 = (f32[768,768]{1,0:T(8,128)}, f32[768,768]{1,0:T(8,128)}, bf16[2,2,8,48,1536]{4,3,2,1,0:T(8,128)(2,1)}, bf16[2,8,48,384]{3,2,1,0:T(8,128)(2...) custom-call(bf16[768,768]{1,0:T(8,128)(2,1)} %refs_0_.3, bf16[768,768]{1,0:T(8,128)(2,1)} %refs_1_.3, ...), custom_call_target="tpu_custom_call" | custom-call | tf_op jit(solution)/shard_map/mlp_and_backward/pallas_call | solution.py:647
  211.9 11.3 %widen.1 = (f32[768,1024]{1,0:T(8,128)}, f32[768,1024]{1,0:T(8,128)}, f32[1024,768]{1,0:T(8,128)}, f32[384,768]{1,0:T(8,128)}, f32[768,384]{1,0:T(8,128)}, /*ind...) custom-call(bf16[2,768,1536]{2,1,0:T(8,128)(2,1)} %bitcast.3, ...), custom_call_target="tpu_custom_call" | custom-call | tf_op jit(solution)/shard_map/widen/pallas_call | solution.py:675

commit v2 on v1

--- a/solution.py
+++ b/solution.py
@@ -373,18 +373,18 @@
 "p2j0":[("C","first",1),("C","rs",0,1),("N","ag",0,1)],
 "p2j1":[("O","rs",0,2)],
 "p2j3":[("C","rs",1,0),("M","ag",0,2)],
-"p2e":[("C","rs",0,2),("N","ag",0,2),("O","rs",0,3),("O","agstart",0)],
-"t0":[("C","rs",0,3),("C","agstart",0),("C","rs",1,1),("M","ag",0,3)],
-"t1":[("C","first",2),("N","ag",0,3),("O","ag",0,0)],
+"p2e":[("C","rs",0,2),("O","rs",0,3),("O","agstart",0)],
+"t0":[("C","rs",0,3),("C","agstart",0),("C","rs",1,1),("N","ag",0,2)],
+"t1":[("C","first",2),("O","ag",0,0)],
 "t2":[("C","rs",1,2)],
 "u0":[("C","rs",2,0),("C","ag",0,0)],
 "u1":[("C","rs",1,3),("C","agstart",1),("O","ag",0,1)],
 "g":[("C","rs",2,1),("C","ag",0,1),("O","ag",0,2)],
 "g0":[("C","rs",2,2),("C","ag",1,0),("C","ag",0,2)],
-"g1":[("C","rs",2,3),("C","agstart",2),("C","ag",1,1),("C","ag",0,3),("O","ag",0,3)],
-"g2":[("C","ag",2,0),("C","ag",1,2)],
-"g3":[("C","ag",2,1),("C","ag",1,3)],
-"z":[("C","ag",2,2),("C","ag",2,3)],
+"g1":[("C","rs",2,3),("C","agstart",2),("C","ag",1,1)],
+"g2":[("C","ag",2,0),("C","ag",1,2),("M","ag",0,3)],
+"g3":[("C","ag",2,1),("N","ag",0,3)],
+"z":[("C","ag",2,2),("C","ag",0,3),("C","ag",1,3),("O","ag",0,3),("C","ag",2,3)],
 }
 def main_kernel(nM,nN,nO,nC,*refs):
     refs=list(refs)
@@ -481,7 +481,7 @@
         def post(i,gpart):
             rows=pl.ds(pl.multiple_of(i*W,W),W)
             r=res[rows,:]; d=dn2[rows,:]
-            acc[rows,:]=acc[rows,:]+r
+            snd[rows,:]=(acc[rows,:]+r).astype(BF)
             i2=lax.rsqrt(jnp.mean(r*r,axis=1,keepdims=True)+EPS)
             s=gain_m[...].astype(F32).reshape(1,-1)*d
             dr=og[rows,:].astype(F32)+i2*s-r*(i2*i2*i2)*jnp.mean(s*r,axis=1,keepdims=True)
@@ -492,7 +492,7 @@
             return gpart+jnp.sum(d*r*i2,axis=0,keepdims=True)
         gpart=lax.fori_loop(0,3,post,jnp.zeros((1,Dm),F32))
         c_dh.start()
-        c_out=pltpu.make_async_copy(acc,out_h,lsem.at[10]); c_out.start()
+        c_out=pltpu.make_async_copy(snd,out_h,lsem.at[10]); c_out.start()
         gx[0,1:2]=gpart
         tick("m1")
         def own(i,_):
@@ -627,9 +627,9 @@
             x=x_ref[r].astype(F32)
             i1=lax.rsqrt(jnp.mean(x*x,axis=1,keepdims=True)+EPS)
             s=gain_a[...].astype(F32).reshape(1,-1)*d
-            res[r]=res[r]+i1*s-x*(i1*i1*i1)*jnp.mean(s*x,axis=1,keepdims=True)
+            snd[r]=(res[r]+i1*s-x*(i1*i1*i1)*jnp.mean(s*x,axis=1,keepdims=True)).astype(BF)
         c_gx.wait(); gains_out[...]=gx[2]+gx[3]
-        c_ig=pltpu.make_async_copy(res,ig_h,lsem.at[11]); c_ig.start()
+        c_ig=pltpu.make_async_copy(snd,ig_h,lsem.at[11]); c_ig.start()
         M.finish(0); N.finish(0); O.finish(0)
         for v in range(3): C.finish(v)
         c_ig.wait()
@@ -643,7 +643,7 @@
     scs=[s.scratch() for s in (RING_M,RING_N,RING_O,RING_C)]
     local=[V((R,H),BF),V((T,H),BF),V((R,Dm),F32)]+[V((R,Dm),BF)]*2
     local+=[V((4,8,Dm),F32),V((RING,8,Dm),F32),pltpu.SemaphoreType.DMA((2,7+RING)),pltpu.SemaphoreType.DMA((21,)),pltpu.SemaphoreType.DMA((2,3))]
-    outs=[sd((R,Dm),F32)]*2+[sd((2,2,RING,48,1536),BF),sd((2,RING,48,H),BF),sd((3,2,RING,48,384),BF),sd((8,Dm),F32)]
+    outs=[sd((R,Dm),BF)]*2+[sd((2,2,RING,48,1536),BF),sd((2,RING,48,H),BF),sd((3,2,RING,48,384),BF),sd((8,Dm),F32)]
     return pl.pallas_call(functools.partial(main_kernel,*[len(s) for s in scs]),
         out_shape=tuple(outs), in_specs=[Vs]*8+[N]*len(hbm), out_specs=(N,)*5+(Vs,),
         scratch_shapes=sum(scs,[])+local,
@@ -652,7 +652,7 @@
 
 def widen_kernel(mlp,wo,qkv,y,dx,gains,gate,up,down,out,query,key,value,y_out,dx_out,ga,gm):
     ga[...]=gains[0]; gm[...]=gains[1]
-    y_out[...]=y[...]; dx_out[...]=dx[...]
+    y_out[...]=y[...].astype(F32); dx_out[...]=dx[...].astype(F32)
     F=mlp.shape[2]//3; H=wo.shape[1]; B=mlp.shape[1]
     for q in range(2):
         cs=slice(F*q,F*q+F)

time: 224 us -> 222 us (level)
  no operation moved by 1% of the time
where the time goes in v2:
time: 222 us
  Pallas kernels  221 us (100%)
    pallas_call x1, Pallas kernels, main_call(): pl.pallas_call(functools.partial(main_kernel, *[len(s) for s in scs]), ou...  141 us
    pallas_call x1, Pallas kernels, front(): pl.pallas_call(functools.partial(front_kernel, nseg), out_shape=(sd((R, D...  68.7 us
    pallas_call x1, Pallas kernels, widen(): pl.pallas_call(widen_kernel, grid=(Dm // B,), out_shape=(sd((Dm, 2 * F),...  11 us

profile of v2, /device:TPU:0, one launch (start us, length us, event | category | flops | bytes accessed | tf_op | source)
XLA Modules:
  0.0 221.8 jit_solution(4167268757519250583)
XLA Ops:
  0.6 68.7 %attention_forward.1 = (bf16[768,768]{1,0:T(8,128)(2,1)}, bf16[1536,768]{1,0:T(8,128)(2,1)}, f32[1536,128]{1,0:T(8,128)}, f32[1536,128]{1,0:T(8,128)}, bf16[6,15...) custom-call(s32[1,7]{1,0:T(1,128)} %starts.1, ...), custom_call_target="tpu_custom_call" | custom-call | tf_op jit(solution)/shard_map/attention_forward/pallas_call | solution.py:227
  69.4 141.2 %mlp_and_backward.1 = (bf16[768,768]{1,0:T(8,128)(2,1)}, bf16[768,768]{1,0:T(8,128)(2,1)}, bf16[2,2,8,48,1536]{4,3,2,1,0:T(8,128)(2,1)}, bf16[2,8,48,384]{3,2,1,...) custom-call(bf16[768,768]{1,0:T(8,128)(2,1)} %refs_0_.3, bf16[768,768]{1,0:T(8,128)(2,1)} %refs_1_.3, ...), custom_call_target="tpu_custom_call" | custom-call | tf_op jit(solution)/shard_map/mlp_and_backward/pallas_call | solution.py:647
  210.6 11.0 %widen.1 = (f32[768,1024]{1,0:T(8,128)}, f32[768,1024]{1,0:T(8,128)}, f32[1024,768]{1,0:T(8,128)}, f32[384,768]{1,0:T(8,128)}, f32[768,384]{1,0:T(8,128)}, /*ind...) custom-call(bf16[2,768,1536]{2,1,0:T(8,128)(2,1)} %bitcast.3, ...), custom_call_target="tpu_custom_call" | custom-call | tf_op jit(solution)/shard_map/widen/pallas_call | solution.py:675

commit v3 on v2

--- a/solution.py
+++ b/solution.py
@@ -374,17 +374,17 @@
 "p2j1":[("O","rs",0,2)],
 "p2j3":[("C","rs",1,0),("M","ag",0,2)],
 "p2e":[("C","rs",0,2),("O","rs",0,3),("O","agstart",0)],
-"t0":[("C","rs",0,3),("C","agstart",0),("C","rs",1,1),("N","ag",0,2)],
-"t1":[("C","first",2),("O","ag",0,0)],
-"t2":[("C","rs",1,2)],
-"u0":[("C","rs",2,0),("C","ag",0,0)],
-"u1":[("C","rs",1,3),("C","agstart",1),("O","ag",0,1)],
-"g":[("C","rs",2,1),("C","ag",0,1),("O","ag",0,2)],
-"g0":[("C","rs",2,2),("C","ag",1,0),("C","ag",0,2)],
-"g1":[("C","rs",2,3),("C","agstart",2),("C","ag",1,1)],
-"g2":[("C","ag",2,0),("C","ag",1,2),("M","ag",0,3)],
-"g3":[("C","ag",2,1),("N","ag",0,3)],
-"z":[("C","ag",2,2),("C","ag",0,3),("C","ag",1,3),("O","ag",0,3),("C","ag",2,3)],
+"t0":[("C","rs",0,3),("C","agstart",0),("N","ag",0,2)],
+"t1":[("C","first",2),("C","rs",1,1)],
+"u0":[("C","rs",2,0),("C","rs",1,2),("O","ag",0,0)],
+"u1":[("C","rs",2,1),("C","ag",0,0)],
+"u2":[("C","rs",1,3),("C","agstart",1)],
+"g":[("C","rs",2,2),("O","ag",0,1)],
+"g0":[("C","rs",2,3),("C","agstart",2),("C","ag",0,1)],
+"g1":[("C","ag",1,0),("O","ag",0,2)],
+"g2":[("C","ag",2,0),("C","ag",1,1),("C","ag",0,2)],
+"g3":[("C","ag",2,1),("C","ag",1,2),("M","ag",0,3)],
+"z":[("C","ag",2,2),("N","ag",0,3),("C","ag",0,3),("C","ag",1,3),("O","ag",0,3),("C","ag",2,3)],
 }
 def main_kernel(nM,nN,nO,nC,*refs):
     refs=list(refs)

time: 222 us -> 222 us (level)
  no operation moved by 1% of the time
where the time goes in v3:
time: 222 us
  Pallas kernels  221 us (100%)
    pallas_call x1, Pallas kernels, main_call(): pl.pallas_call(functools.partial(main_kernel, *[len(s) for s in scs]), ou...  141 us
    pallas_call x1, Pallas kernels, front(): pl.pallas_call(functools.partial(front_kernel, nseg), out_shape=(sd((R, D...  68.7 us
    pallas_call x1, Pallas kernels, widen(): pl.pallas_call(widen_kernel, grid=(Dm // B,), out_shape=(sd((Dm, 2 * F),...  11 us

profile of v3, /device:TPU:0, one launch (start us, length us, event | category | flops | bytes accessed | tf_op | source)
XLA Modules:
  0.0 221.9 jit_solution(10257521049159704965)
XLA Ops:
  0.6 68.7 %attention_forward.1 = (bf16[768,768]{1,0:T(8,128)(2,1)}, bf16[1536,768]{1,0:T(8,128)(2,1)}, f32[1536,128]{1,0:T(8,128)}, f32[1536,128]{1,0:T(8,128)}, bf16[6,15...) custom-call(s32[1,7]{1,0:T(1,128)} %starts.1, ...), custom_call_target="tpu_custom_call" | custom-call | tf_op jit(solution)/shard_map/attention_forward/pallas_call | solution.py:227
  69.4 141.3 %mlp_and_backward.1 = (bf16[768,768]{1,0:T(8,128)(2,1)}, bf16[768,768]{1,0:T(8,128)(2,1)}, bf16[2,2,8,48,1536]{4,3,2,1,0:T(8,128)(2,1)}, bf16[2,8,48,384]{3,2,1,...) custom-call(bf16[768,768]{1,0:T(8,128)(2,1)} %refs_0_.3, bf16[768,768]{1,0:T(8,128)(2,1)} %refs_1_.3, ...), custom_call_target="tpu_custom_call" | custom-call | tf_op jit(solution)/shard_map/mlp_and_backward/pallas_call | solution.py:647
  210.7 11.0 %widen.1 = (f32[768,1024]{1,0:T(8,128)}, f32[768,1024]{1,0:T(8,128)}, f32[1024,768]{1,0:T(8,128)}, f32[384,768]{1,0:T(8,128)}, f32[768,384]{1,0:T(8,128)}, /*ind...) custom-call(bf16[2,768,1536]{2,1,0:T(8,128)(2,1)} %bitcast.3, ...), custom_call_target="tpu_custom_call" | custom-call | tf_op jit(solution)/shard_map/widen/pallas_call | solution.py:675
